TPU v7x, 32 devices: a whole 2x2x4 slice. The times are simulated.
32 devices in a mesh: expert: 4 (over y, core), fsdp: 8 (over z, x).
Axes of the slice: x: 2, y: 2, z: 4, core: 2. Of those that a mesh axis runs over, the one named last changes fastest.
Arguments:
- layer_input: bfloat16 [8192, 2048], P(('expert', 'fsdp')), may hold values from -6 to 6
- expert_ids: int32 [8192, 8], P(('expert', 'fsdp')), may hold values from 0 to 15, as said below
- slot_ids: int32 [8192, 8], P(('expert', 'fsdp')), may hold values from 0 to 255, as said below
- attn_gain: float32 [2048], replicated, may hold values from 0.25 to 1.75
- qkv_weight: bfloat16 [2048, 6144], P('fsdp'), may hold values from -0.125 to 0.125
- query_gain: float32 [128], replicated, may hold values from 0.25 to 1.75
- key_gain: float32 [128], replicated, may hold values from 0.25 to 1.75
- out_weight: bfloat16 [2048, 2048], P('fsdp'), may hold values from -1 to 1
- ffn_gain: float32 [2048], replicated, may hold values from 0.25 to 1.75
- router_weight: bfloat16 [2048, 16], P('fsdp'), may hold values from -0.0625 to 0.0625
- gate_up_weight: bfloat16 [16, 2048, 2048], P('expert', 'fsdp'), may hold values from -0.125 to 0.125
- down_weight: bfloat16 [16, 1024, 2048], P('expert', 'fsdp'), may hold values from -0.75 to 0.75
- cotangent: bfloat16 [8192, 2048], P(('expert', 'fsdp')), may hold values from -6 to 6
Outputs:
- mixed_out: bfloat16 [8192, 2048], P(('expert', 'fsdp'))
- input_grad: float32 [8192, 2048], P(('expert', 'fsdp'))
- attn_gain_grad: float32 [2048], replicated
- qkv_weight_grad: float32 [2048, 6144], P('fsdp')
- query_gain_grad: float32 [128], replicated
- key_gain_grad: float32 [128], replicated
- out_weight_grad: float32 [2048, 2048], P('fsdp')
- ffn_gain_grad: float32 [2048], replicated
- router_weight_grad: float32 [2048, 16], P('fsdp')
- gate_up_grad: float32 [16, 2048, 2048], P('expert', 'fsdp')
- down_grad: float32 [16, 1024, 2048], P('expert', 'fsdp')
Inputs may be any that keep to these rules, and one draw needn't show every extreme that they name: `expert_ids`: each row names 8 different experts. Among the 256 rows of one device no expert is named more than 256 times; in every device's rows one expert is named exactly 256 times. `slot_ids`: among the rows of one device, the routes to one expert have different slots.
All inputs are finite; a program needn't handle non-finite values.
Results may differ from a plain program's by a relative error of at most 0.022.
Values may be sent and summed in bfloat16 or wider, within the bound.
No kernel may reach another device: no remote copies, remote signals or barrier semaphores. Data moves between devices by JAX's collectives and lax.ppermute only.
A program may use at most 384 MiB of HBM per device.

v0:
```python
import jax
import jax.numpy as jnp
from jax import lax
from jax.sharding import PartitionSpec as P

EPSILON = 1e-06
ROPE_BASE = 50000.0


def normalize(values):
    factor = lax.rsqrt(jnp.mean(values * values, -1, keepdims=True) + EPSILON)
    return (values * factor, factor)


def norm_back(grad_unit, unit_val, factor):
    return factor * (grad_unit - unit_val * jnp.mean(grad_unit * unit_val, -1, keepdims=True))


def tables(length, head_size):
    half_size = head_size // 2
    frequency = ROPE_BASE ** (-(jnp.arange(half_size, dtype=jnp.float32) * 2.0 / head_size))
    angles = jnp.arange(length, dtype=jnp.float32)[:, None] * frequency[None, :]
    angles = jnp.concatenate([angles, angles], 1)
    return (jnp.cos(angles)[:, None, :], jnp.sin(angles)[:, None, :])


def rotate(values, cos_table, sine_table):
    half_size = values.shape[-1] // 2
    turned = jnp.concatenate([-values[..., half_size:], values[..., :half_size]], -1)
    return values * cos_table + turned * sine_table


def rotate_back(gradient, cos_table, sine_table):
    half_size = gradient.shape[-1] // 2
    turned_grad = gradient * sine_table
    return gradient * cos_table + jnp.concatenate(
        [turned_grad[..., half_size:], -turned_grad[..., :half_size]], -1
    )


def local(
    layer_input,
    expert_ids,
    slot_ids,
    attn_gain,
    qkv_weight,
    query_gain,
    key_gain,
    out_weight,
    ffn_gain,
    router_weight,
    gate_up_weight,
    down_weight,
    cotangent,
):
    tokens, model_width = layer_input.shape
    top_count = expert_ids.shape[1]
    head_size = query_gain.shape[0]
    head_count = model_width // head_size
    experts = router_weight.shape[1]
    hidden = gate_up_weight.shape[2] // 2
    capacity = 2 * tokens * top_count // experts
    score_scale = head_size ** (-0.5)
    source = layer_input.astype(jnp.float32)
    unit_one, factor_one = normalize(source)
    normed = (unit_one * attn_gain).astype(jnp.bfloat16)
    qkv_full, out_full, router_full = (
        lax.all_gather(qkv_weight, "fsdp", axis=0, tiled=True),
        lax.all_gather(out_weight, "fsdp", axis=0, tiled=True),
        lax.all_gather(router_weight, "fsdp", axis=0, tiled=True),
    )
    projected = jnp.dot(normed, qkv_full, preferred_element_type=jnp.float32)
    queries = projected[:, :model_width].reshape(tokens, head_count, head_size)
    keys_raw = projected[:, model_width : 2 * model_width].reshape(tokens, head_count, head_size)
    values_raw = projected[:, 2 * model_width :].reshape(tokens, head_count, head_size)
    unit_query, factor_query = normalize(queries)
    unit_key, factor_key = normalize(keys_raw)
    cos_table, sine_table = tables(tokens, head_size)
    query_rot = rotate(unit_query * query_gain, cos_table, sine_table).astype(jnp.bfloat16)
    key_rot = rotate(unit_key * key_gain, cos_table, sine_table).astype(jnp.bfloat16)
    value_low = values_raw.astype(jnp.bfloat16)
    scores = (
        jnp.einsum("qhd,khd->hqk", query_rot, key_rot, preferred_element_type=jnp.float32)
        * score_scale
    )
    top_score = jnp.max(scores, -1, keepdims=True)
    weights_raw = jnp.exp(scores - top_score)
    totals = jnp.sum(weights_raw, -1, keepdims=True)
    log_total = top_score + jnp.log(totals)
    prob_low = (weights_raw / totals).astype(jnp.bfloat16)
    mixed_heads = jnp.einsum(
        "hqk,khd->qhd", prob_low, value_low, preferred_element_type=jnp.float32
    )
    mixed_low = mixed_heads.reshape(tokens, model_width).astype(jnp.bfloat16)
    residual = source + jnp.dot(mixed_low, out_full, preferred_element_type=jnp.float32)
    unit_two, factor_two = normalize(residual)
    normed_two = (unit_two * ffn_gain).astype(jnp.bfloat16)
    logits = jnp.dot(normed_two, router_full, preferred_element_type=jnp.float32)
    onehot = (expert_ids[:, :, None] == jnp.arange(experts, dtype=jnp.int32)[None, None, :]).astype(
        jnp.float32
    )
    chosen = jnp.sum(onehot * logits[:, None, :], -1)
    gate_probs = jax.nn.softmax(chosen, -1)
    slot_index = (expert_ids * capacity + slot_ids).reshape(-1)
    copies = jnp.broadcast_to(normed_two[:, None, :], (tokens, top_count, model_width)).reshape(
        tokens * top_count, model_width
    )
    outgoing = jnp.zeros((experts * capacity, model_width), jnp.bfloat16).at[slot_index].set(copies)
    arrived = lax.all_to_all(
        outgoing.reshape(experts, capacity, model_width),
        "expert",
        split_axis=0,
        concat_axis=1,
        tiled=True,
    )
    gate_up_full, down_full = (
        lax.all_gather(gate_up_weight, "fsdp", axis=1, tiled=True),
        lax.all_gather(down_weight, "fsdp", axis=1, tiled=True),
    )
    gate_up_val = jnp.einsum(
        "erd,edf->erf", arrived, gate_up_full, preferred_element_type=jnp.float32
    )
    gate_part = gate_up_val[..., :hidden]
    up_part = gate_up_val[..., hidden:]
    sigmoid_gate = jax.nn.sigmoid(gate_part)
    activated = (gate_part * sigmoid_gate * up_part).astype(jnp.bfloat16)
    expert_out = jnp.einsum(
        "erf,efd->erd", activated, down_full, preferred_element_type=jnp.float32
    ).astype(jnp.bfloat16)
    returned = lax.all_to_all(
        expert_out, "expert", split_axis=1, concat_axis=0, tiled=True
    ).reshape(experts * capacity, model_width)
    picked = returned[slot_index].reshape(tokens, top_count, model_width).astype(jnp.float32)
    moe_sum = jnp.sum(gate_probs[:, :, None] * picked, 1)
    mixed_out = (residual + moe_sum).astype(jnp.bfloat16)
    upstream = cotangent.astype(jnp.float32)
    gate_grad = jnp.sum(picked * upstream[:, None, :], -1)
    row_grad = (
        (gate_probs[:, :, None] * upstream[:, None, :])
        .astype(jnp.bfloat16)
        .reshape(tokens * top_count, model_width)
    )
    grad_out = (
        jnp.zeros((experts * capacity, model_width), jnp.bfloat16).at[slot_index].set(row_grad)
    )
    grad_arrived = lax.all_to_all(
        grad_out.reshape(experts, capacity, model_width),
        "expert",
        split_axis=0,
        concat_axis=1,
        tiled=True,
    )
    gate_up_back, down_back = (
        lax.all_gather(gate_up_weight, "fsdp", axis=1, tiled=True),
        lax.all_gather(down_weight, "fsdp", axis=1, tiled=True),
    )
    act_grad = jnp.einsum(
        "erd,efd->erf", grad_arrived, down_back, preferred_element_type=jnp.float32
    )
    down_grad_full = jnp.einsum(
        "erf,erd->efd", activated, grad_arrived, preferred_element_type=jnp.float32
    )
    gate_grad_part = act_grad * up_part * sigmoid_gate * (1.0 + gate_part * (1.0 - sigmoid_gate))
    up_grad_part = act_grad * gate_part * sigmoid_gate
    both_grad = jnp.concatenate([gate_grad_part, up_grad_part], -1).astype(jnp.bfloat16)
    gate_up_grad_full = jnp.einsum(
        "erd,erf->edf", arrived, both_grad, preferred_element_type=jnp.float32
    )
    input_rows = jnp.einsum(
        "erf,edf->erd", both_grad, gate_up_back, preferred_element_type=jnp.float32
    ).astype(jnp.bfloat16)
    rows_back = lax.all_to_all(
        input_rows, "expert", split_axis=1, concat_axis=0, tiled=True
    ).reshape(experts * capacity, model_width)
    gate_up_grad, down_grad = (
        lax.psum_scatter(
            gate_up_grad_full.astype(jnp.bfloat16), "fsdp", scatter_dimension=1, tiled=True
        ).astype(jnp.float32),
        lax.psum_scatter(
            down_grad_full.astype(jnp.bfloat16), "fsdp", scatter_dimension=1, tiled=True
        ).astype(jnp.float32),
    )
    mean_grad = jnp.sum(gate_probs * gate_grad, -1, keepdims=True)
    chosen_grad = gate_probs * (gate_grad - mean_grad)
    logit_grad = jnp.sum(onehot * chosen_grad[:, :, None], 1).astype(jnp.bfloat16)
    router_grad_full = jnp.dot(normed_two.T, logit_grad, preferred_element_type=jnp.float32)
    routed_back = jnp.sum(
        rows_back[slot_index].reshape(tokens, top_count, model_width).astype(jnp.float32), 1
    )
    normed_two_grad = routed_back + jnp.dot(
        logit_grad, router_full.T, preferred_element_type=jnp.float32
    )
    ffn_gain_part = jnp.sum(normed_two_grad * unit_two, 0)
    residual_grad = upstream + norm_back(normed_two_grad * ffn_gain, unit_two, factor_two)
    attn_grad_low = residual_grad.astype(jnp.bfloat16)
    out_grad_full = jnp.dot(mixed_low.T, attn_grad_low, preferred_element_type=jnp.float32)
    mixed_grad = jnp.dot(attn_grad_low, out_full.T, preferred_element_type=jnp.float32).astype(
        jnp.bfloat16
    )
    mixed_grad = mixed_grad.reshape(tokens, head_count, head_size)
    value_grad = jnp.einsum(
        "hqk,qhd->khd", prob_low, mixed_grad, preferred_element_type=jnp.float32
    )
    prob_grad = jnp.einsum(
        "qhd,khd->hqk", mixed_grad, value_low, preferred_element_type=jnp.float32
    )
    scores_again = (
        jnp.einsum("qhd,khd->hqk", query_rot, key_rot, preferred_element_type=jnp.float32)
        * score_scale
    )
    prob_full = jnp.exp(scores_again - log_total)
    score_grad = (
        prob_full * (prob_grad - jnp.sum(prob_full * prob_grad, -1, keepdims=True))
    ).astype(jnp.bfloat16)
    query_grad = (
        jnp.einsum("hqk,khd->qhd", score_grad, key_rot, preferred_element_type=jnp.float32)
        * score_scale
    )
    key_grad = (
        jnp.einsum("hqk,qhd->khd", score_grad, query_rot, preferred_element_type=jnp.float32)
        * score_scale
    )
    query_grad = rotate_back(query_grad, cos_table, sine_table)
    key_grad = rotate_back(key_grad, cos_table, sine_table)
    query_gain_part = jnp.sum(query_grad * unit_query, (0, 1))
    key_gain_part = jnp.sum(key_grad * unit_key, (0, 1))
    query_pre = norm_back(query_grad * query_gain, unit_query, factor_query)
    key_pre = norm_back(key_grad * key_gain, unit_key, factor_key)
    qkv_grad_low = jnp.concatenate(
        [
            query_pre.reshape(tokens, model_width),
            key_pre.reshape(tokens, model_width),
            value_grad.reshape(tokens, model_width),
        ],
        1,
    ).astype(jnp.bfloat16)
    qkv_grad_full = jnp.dot(normed.T, qkv_grad_low, preferred_element_type=jnp.float32)
    normed_grad = jnp.dot(qkv_grad_low, qkv_full.T, preferred_element_type=jnp.float32)
    attn_gain_part = jnp.sum(normed_grad * unit_one, 0)
    input_grad = residual_grad + norm_back(normed_grad * attn_gain, unit_one, factor_one)
    qkv_shard, out_shard, router_shard = (
        lax.psum_scatter(
            qkv_grad_full.astype(jnp.bfloat16), "fsdp", scatter_dimension=0, tiled=True
        ).astype(jnp.float32),
        lax.psum_scatter(
            out_grad_full.astype(jnp.bfloat16), "fsdp", scatter_dimension=0, tiled=True
        ).astype(jnp.float32),
        lax.psum_scatter(
            router_grad_full.astype(jnp.bfloat16), "fsdp", scatter_dimension=0, tiled=True
        ).astype(jnp.float32),
    )
    qkv_weight_grad, out_weight_grad, router_weight_grad = (
        lax.psum(qkv_shard.astype(jnp.bfloat16), "expert").astype(jnp.float32),
        lax.psum(out_shard.astype(jnp.bfloat16), "expert").astype(jnp.float32),
        lax.psum(router_shard.astype(jnp.bfloat16), "expert").astype(jnp.float32),
    )
    attn_gain_grad, query_gain_grad, key_gain_grad, ffn_gain_grad = lax.psum(
        (attn_gain_part, query_gain_part, key_gain_part, ffn_gain_part), ("expert", "fsdp")
    )
    return (
        mixed_out,
        input_grad,
        attn_gain_grad,
        qkv_weight_grad,
        query_gain_grad,
        key_gain_grad,
        out_weight_grad,
        ffn_gain_grad,
        router_weight_grad,
        gate_up_grad,
        down_grad,
    )


def solution(mesh):
    return jax.shard_map(
        local,
        mesh=mesh,
        in_specs=(
            P(("expert", "fsdp"), None),
            P(("expert", "fsdp"), None),
            P(("expert", "fsdp"), None),
            P(),
            P("fsdp", None),
            P(),
            P(),
            P("fsdp", None),
            P(),
            P("fsdp", None),
            P("expert", "fsdp", None),
            P("expert", "fsdp", None),
            P(("expert", "fsdp"), None),
        ),
        out_specs=(
            P(("expert", "fsdp"), None),
            P(("expert", "fsdp"), None),
            P(),
            P("fsdp", None),
            P(),
            P(),
            P("fsdp", None),
            P(),
            P("fsdp", None),
            P("expert", "fsdp", None),
            P("expert", "fsdp", None),
        ),
        check_vma=False,
    )
```

profile of v0, /device:TPU:0, one launch (start us, length us, event | category | flops | bytes accessed | tf_op | source)
XLA Modules:
  0.0 3566.4 jit_solution(18210329636455333657)
XLA Ops:
  11.3 67.9 %all_gather.19 = bf16[2048,16]{0,1:T(8,128)(2,1)S(1)} all-gather(bf16[256,16]{0,1:T(8,128)(2,1)S(1)} %copy-done.66), channel_id=1, replica_groups=mesh['expert'=4,'fsdp'=8] {'fsdp'}, dimensions={0}, use_global_device_ids=true | all-gather | bytes 73728 | tf_op jit(solution)/shard_map/all_gather | solution.py:70
  80.8 413.0 %all-gather.5.cloned.1.call-done = bf16[2048,6144]{1,0:T(8,128)(2,1)} async-done(((bf16[256,6144]{1,0:T(8,128)(2,1)}), bf16[2048,6144]{1,0:T(8,128)(2,1)}) %all-gather.5.cloned.1.call-update) | async-done | bytes 25165840 | tf_op jit(solution)/shard_map/all_gather | solution.py:68
  537.7 83.1 %all-gather.7.cloned.1.call-done = bf16[2048,2048]{1,0:T(8,128)(2,1)} async-done(((bf16[256,2048]{1,0:T(8,128)(2,1)}), bf16[2048,2048]{1,0:T(8,128)(2,1)}) %all-gather.7.cloned.1.call-update) | async-done | bytes 8388624 | tf_op jit(solution)/shard_map/all_gather | solution.py:69
  629.6 22.2 scatter_custom_fusion.1
  680.6 161.2 %all-to-all-done.2 = bf16[16,256,2048]{2,1,0:T(8,128)(2,1)} async-done(((bf16[16,256,2048]{2,1,0:T(8,128)(2,1)}), bf16[16,256,2048]{2,1,0:T(8,128)(2,1)}, u32[]{:S(2)}, u32[]{:S(2)}) %all-to-all-start.2) | async-done | bytes 16777248 | tf_op jit(solution)/shard_map/all_to_all | solution.py:146
  863.7 168.8 %all-to-all-done = bf16[16,256,2048]{2,1,0:T(8,128)(2,1)} async-done(((bf16[16,256,2048]{2,1,0:T(8,128)(2,1)}), bf16[16,256,2048]{2,1,0:T(8,128)(2,1)}, u32[]{:S(2)}, u32[]{:S(2)}) %all-to-all-start) | async-done | bytes 16777248 | tf_op jit(solution)/shard_map/all_to_all | solution.py:109
  1046.7 211.6 %all-gather.9.cloned.1.call-done = bf16[4,2048,2048]{2,1,0:T(8,128)(2,1)} async-done(((bf16[4,256,2048]{2,1,0:T(8,128)(2,1)}), bf16[4,2048,2048]{2,1,0:T(8,128)(2,1)}) %all-gather.9.cloned.1.call-update) | async-done | bytes 33554448 | tf_op jit(solution)/shard_map/all_gather | solution.py:117
  1258.3 43.2 %fusion.53 = f32[4,1024,2048]{2,1,0:T(8,128)} fusion(bf16[4,1024,2048]{2,1,0:T(8,128)(2,1)} %bitcast.118, bf16[4,2048,2048]{2,1,0:T(8,128)(2,1)} %all-gather.9.cloned.1.call-done), kind=kOutput, calls=%fused_computation.138 | convolution fusion | flops 34359738368 | bytes 83886080 | tf_op jit(solution)/shard_map/erd,edf->erf/dot_general | solution.py:120
  1301.5 186.5 %all-gather.11.cloned.1.call-done = bf16[4,1024,2048]{2,1,0:T(8,128)(2,1)} async-done(((bf16[4,128,2048]{2,1,0:T(8,128)(2,1)}), bf16[4,1024,2048]{2,1,0:T(8,128)(2,1)}) %all-gather.11.cloned.1.call-update) | async-done | bytes 16777232 | tf_op jit(solution)/shard_map/all_gather | solution.py:118
  1488.0 37.0 %multiply_convert_fusion.1 = (bf16[4,1024,1024]{2,1,0:T(8,128)(2,1)}, bf16[4,1024,1024]{2,1,0:T(8,128)(2,1)}, bf16[4,1024,1024]{2,1,0:T(8,128)(2,1)}) fusion(f32[4,1024,2048]{2,1,0:T(8,128)} %fusion.53, bf16[4,1024,2048]{2,1,0:T(8,128)(2,1)} %bitcast.120, bf16[4,1024,2048]{2,1,0:T(8,128)(2,1)} %all-gather.11.cloned.1.call-done), kind=kOutput, calls=%fused_computation.15 | convolution fusion | flops 17246978048 | bytes 92274688 | tf_op jit(solution)/shard_map/erd,efd->erf/dot_general | solution.py:157
  1525.0 27.2 convolution_convert_fusion.4
  1581.4 43.4 %convolution_convert_fusion.2 = bf16[4,1024,2048]{2,1,0:T(8,128)(2,1)} fusion(bf16[4,2048,2048]{2,1,0:T(8,128)(2,1)} %all-gather.9.cloned.1.call-done, bf16[4,1024,1024]{2,1,0:T(8,128)(2,1)} %get-tuple-element.30, bf16[4,1024,1024]{2,1,0:T(8,128)(2,1)} %get-tuple-element.29), kind=kOutput, calls=%fused_computation.18 | convolution fusion | flops 34401681408 | bytes 67108864 | tf_op jit(solution)/shard_map/erf,edf->erd/dot_general | solution.py:169
  1646.9 117.5 %all-to-all-done.1 = bf16[4,1024,2048]{2,0,1:T(4,128)(2,1)} async-done(((bf16[4,1024,2048]{2,0,1:T(4,128)(2,1)}), bf16[4,1024,2048]{2,0,1:T(4,128)(2,1)}, u32[]{:S(2)}, u32[]{:S(2)}) %all-to-all-start.1) | async-done | bytes 16777248 | tf_op jit(solution)/shard_map/all_to_all | solution.py:130
  1790.4 24.4 gather_fusion
  1824.5 130.2 %all-to-all-done.3 = bf16[4,1024,2048]{2,0,1:T(4,128)(2,1)} async-done(((bf16[4,1024,2048]{2,0,1:T(4,128)(2,1)}), bf16[4,1024,2048]{2,0,1:T(4,128)(2,1)}, u32[]{:S(2)}, u32[]{:S(2)}) %all-to-all-start.3) | async-done | bytes 16777248 | tf_op jit(solution)/shard_map/all_to_all | solution.py:172
  1973.3 24.6 gather_fusion.1
  2061.9 27.1 convolution_convert_fusion.3
  2089.1 78.6 %reduce-scatter.8.cloned.1.call-done = bf16[256,2048]{1,0:T(8,128)(2,1)} async-done(((bf16[2048,2048]{1,0:T(8,128)(2,1)}), bf16[256,2048]{1,0:T(8,128)(2,1)}) %reduce-scatter.8.cloned.1.call-update) | async-done | bytes 1048592 | tf_op jit(solution)/shard_map/reduce_scatter | solution.py:245
  2167.7 407.0 %reduce-scatter.6.cloned.1.call-done = bf16[256,6144]{1,0:T(8,128)(2,1)} async-done(((bf16[2048,6144]{1,0:T(8,128)(2,1)}), bf16[256,6144]{1,0:T(8,128)(2,1)}) %reduce-scatter.6.cloned.1.call-update) | async-done | bytes 3145744 | tf_op jit(solution)/shard_map/reduce_scatter | solution.py:242
  2574.8 43.8 %convolution_convert_fusion = bf16[4,2048,2048]{2,1,0:T(8,128)(2,1)} fusion(bf16[4,1024,2048]{2,1,0:T(8,128)(2,1)} %bitcast.119, bf16[4,1024,1024]{2,1,0:T(8,128)(2,1)} %get-tuple-element.30, bf16[4,1024,1024]{2,1,0:T(8,128)(2,1)} %get-tuple-element.29), kind=kOutput, calls=%fused_computation.4 | convolution fusion | flops 34410070016 | bytes 67108864 | tf_op jit(solution)/shard_map/erd,erf->edf/dot_general | solution.py:166
  2633.0 43.8 %all-reduce = (f32[2048]{0:T(1024)}, f32[128]{0:T(128)}, f32[128]{0:T(128)}, f32[2048]{0:T(1024)}) all-reduce(f32[2048]{0:T(1024)S(1)} %get-tuple-element.19, f32[128]{0:T(128)S(1)} %copy-done.71, f32[128]{0:T(128)S(1)} %copy-done.72, f32[2048]{0:T(1024)S(1)} %copy-done.56), channel_id=1, replica_groups=mesh['expert'=4,'fsdp'=8] {'expert','fsdp'}, use_global_device_ids=true, to_apply=%region_22.0 | all-reduce | flops 4352 | bytes 34816 | tf_op jit(solution)/shard_map/psum | solution.py:257
  2687.6 230.5 %reduce-scatter.14.cloned.1.call-done = bf16[4,128,2048]{2,1,0:T(8,128)(2,1)} async-done(((bf16[4,1024,2048]{2,1,0:T(8,128)(2,1)}), bf16[4,128,2048]{2,1,0:T(8,128)(2,1)}) %reduce-scatter.14.cloned.1.call-update) | async-done | bytes 2097168 | tf_op jit(solution)/shard_map/reduce_scatter | solution.py:179
  2922.2 83.0 %all-reduce.4.cloned.1.call-done = (bf16[256,6144]{1,0:T(8,128)(2,1)}, bf16[256,2048]{1,0:T(8,128)(2,1)}) async-done(((bf16[256,6144]{1,0:T(8,128)(2,1)}, bf16[256,2048]{1,0:T(8,128)(2,1)}), (bf16[256,6144]{1,0:T(8,128)(2,1)}, bf16[256,2048]{1,0:T(8,128)(2,1)})) %all-reduce.4.cloned.1.call-update) | async-done | bytes 4194320 | tf_op jit(solution)/shard_map/psum | solution.py:253
  3011.6 541.0 %reduce-scatter.12.cloned.1.call-done = bf16[4,256,2048]{2,1,0:T(8,128)(2,1)} async-done(((bf16[4,2048,2048]{2,1,0:T(8,128)(2,1)}), bf16[4,256,2048]{2,1,0:T(8,128)(2,1)}) %reduce-scatter.12.cloned.1.call-update) | async-done | bytes 4194320 | tf_op jit(solution)/shard_map/reduce_scatter | solution.py:176
  (255 shorter events, 334.2 us)
Async XLA Ops:
  7.2 486.6 %all-gather.5.cloned.1.call-start = ((), (), s32[]{:S(2)}) async-start(), calls=%async_computation.9 | async-start | bytes 28311552 | tf_op jit(solution)/shard_map/all_gather | solution.py:68
  7.9 612.9 %all-gather.7.cloned.1.call-start = ((), (), s32[]{:S(2)}) async-start(), calls=%async_computation.10 | async-start | bytes 9437184 | tf_op jit(solution)/shard_map/all_gather | solution.py:69
  8.7 71.8 %copy-start.14 = (bf16[256,2048]{1,0:T(8,128)(2,1)S(1)}, bf16[256,2048]{1,0:T(8,128)(2,1)}, u32[]{:S(2)}) copy-start(bf16[256,2048]{1,0:T(8,128)(2,1)} %param.13) | copy-start | bytes 3145732
  8.7 485.1 %copy-start.34 = (f32[2048]{0:T(1024)S(1)}, f32[2048]{0:T(1024)}, u32[]{:S(2)}) copy-start(f32[2048]{0:T(1024)} %param.16) | copy-start | bytes 24580
  8.7 1249.6 %all-gather.9.cloned.1.call-start = ((), (), s32[]{:S(2)}) async-start(), calls=%async_computation.11 | async-start | bytes 37748736 | tf_op jit(solution)/shard_map/all_gather | solution.py:117
  79.2 549.1 %copy-start.36 = (bf16[2048,16]{0,1:T(8,128)(2,1)}, bf16[2048,16]{0,1:T(8,128)(2,1)S(1)}, u32[]{:S(2)}) copy-start(bf16[2048,16]{0,1:T(8,128)(2,1)S(1)} %all_gather.19) | copy-start | bytes 196612
  80.8 424.7 %copy-start.50 = (f32[256]{0:T(256)}, f32[256]{0:T(256)S(1)}, u32[]{:S(2)}) copy-start(f32[256]{0:T(256)S(1)} %add_rsqrt_fusion.3) | copy-start | bytes 3076
  80.8 578.6 %copy-start.57 = (s32[2048,1]{0,1:T(1,128)}, s32[2048,1]{0,1:T(1,128)S(1)}, u32[]{:S(2)}) copy-start(s32[2048,1]{0,1:T(1,128)S(1)} %compare_select_fusion) | copy-start | bytes 24580
  537.7 83.1 %copy-start.18 = (bf16[16,128,256]{2,1,0:T(8,128)(2,1)}, bf16[16,128,256]{2,1,0:T(8,128)(2,1)S(1)}, u32[]{:S(2)}) copy-start(bf16[16,128,256]{2,1,0:T(8,128)(2,1)S(1)} %convolution_convert_fusion.9) | copy-start | bytes 3145732
  626.7 25.1 copy-start.61
  628.3 31.2 copy-start.16
  651.8 190.1 %all-to-all-start.2 = ((bf16[16,256,2048]{2,1,0:T(8,128)(2,1)}), bf16[16,256,2048]{2,1,0:T(8,128)(2,1)}, u32[]{:S(2)}, u32[]{:S(2)}) async-start(bf16[16,256,2048]{2,1,0:T(8,128)(2,1)} %bitcast.113), calls=%async_computation.2 | async-start | bytes 33554432 | tf_op jit(solution)/shard_map/all_to_all | solution.py:146
  658.8 829.2 %all-gather.11.cloned.1.call-start = ((), (), s32[]{:S(2)}) async-start(), calls=%async_computation.12 | async-start | bytes 18874368 | tf_op jit(solution)/shard_map/all_gather | solution.py:118
  841.9 190.6 %all-to-all-start = ((bf16[16,256,2048]{2,1,0:T(8,128)(2,1)}), bf16[16,256,2048]{2,1,0:T(8,128)(2,1)}, u32[]{:S(2)}, u32[]{:S(2)}) async-start(bf16[16,256,2048]{2,1,0:T(8,128)(2,1)} %bitcast.112), calls=%async_computation | async-start | bytes 33554432 | tf_op jit(solution)/shard_map/all_to_all | solution.py:109
  1574.3 190.1 %all-to-all-start.1 = ((bf16[4,1024,2048]{2,0,1:T(4,128)(2,1)}), bf16[4,1024,2048]{2,0,1:T(4,128)(2,1)}, u32[]{:S(2)}, u32[]{:S(2)}) async-start(bf16[4,1024,2048]{2,0,1:T(4,128)(2,1)} %copy.196), calls=%async_computation.1 | async-start | bytes 33554432 | tf_op jit(solution)/shard_map/all_to_all | solution.py:130
  1646.9 124.8 %copy-start.58 = (s32[2048,1]{0,1:T(1,128)S(1)}, s32[2048,1]{0,1:T(1,128)}, u32[]{:S(2)}) copy-start(s32[2048,1]{0,1:T(1,128)} %copy-done.57) | copy-start | bytes 24580
  1764.5 190.3 %all-to-all-start.3 = ((bf16[4,1024,2048]{2,0,1:T(4,128)(2,1)}), bf16[4,1024,2048]{2,0,1:T(4,128)(2,1)}, u32[]{:S(2)}, u32[]{:S(2)}) async-start(bf16[4,1024,2048]{2,0,1:T(4,128)(2,1)} %copy.202), calls=%async_computation.3 | async-start | bytes 33554432 | tf_op jit(solution)/shard_map/all_to_all | solution.py:172
  1771.7 396.0 %reduce-scatter.8.cloned.1.call-start = ((), (), s32[]{:S(2)}) async-start(), calls=%async_computation.14 | async-start | bytes 9437184 | tf_op jit(solution)/shard_map/reduce_scatter | solution.py:245
  2021.3 553.5 %reduce-scatter.6.cloned.1.call-start = ((), (), s32[]{:S(2)}) async-start(), calls=%async_computation.13 | async-start | bytes 28311552 | tf_op jit(solution)/shard_map/reduce_scatter | solution.py:242
  2059.8 620.5 %reduce-scatter.10.cloned.1.call-start = ((), (), s32[]{:S(2)}) async-start(), calls=%async_computation.15 | async-start | bytes 73728 | tf_op jit(solution)/shard_map/reduce_scatter | solution.py:248
  2061.8 856.2 %reduce-scatter.14.cloned.1.call-start = ((), (), s32[]{:S(2)}) async-start(), calls=%async_computation.17 | async-start | bytes 18874368 | tf_op jit(solution)/shard_map/reduce_scatter | solution.py:179
  2089.1 916.2 %all-reduce.4.cloned.1.call-start = ((), (), s32[]{:S(2)}) async-start(), calls=%async_computation.18 | async-start | bytes 8388608 | tf_op jit(solution)/shard_map/psum | solution.py:253
  2574.8 977.9 %reduce-scatter.12.cloned.1.call-start = ((), (), s32[]{:S(2)}) async-start(), calls=%async_computation.16 | async-start | bytes 37748736 | tf_op jit(solution)/shard_map/reduce_scatter | solution.py:176
  2618.7 58.1 %copy-start.9 = (f32[256,2048]{1,0:T(8,128)S(1)}, f32[256,2048]{1,0:T(8,128)}, u32[]{:S(2)}) copy-start(f32[256,2048]{1,0:T(8,128)} %copy-done.7) | copy-start | bytes 6291460
  (63 other events, 344.0 us)
Sparse Core Ops, SparseCore 0:
  9.5 484.1 all-gather.4
  495.9 124.8 all-gather.6
  622.4 635.9 all-gather.8
  1260.4 227.5 all-gather.10
  2021.4 146.2 reduce-scatter.7
  2171.9 402.7 reduce-scatter.5
  2578.2 52.8 reduce-scatter.9
  2635.3 282.7 reduce-scatter.13
  2920.5 84.6 all-reduce.3
  3009.3 543.2 reduce-scatter.11
where the time goes:
time: 3570 us
  waiting for transfers between devices  2810 us (79%)
  matrix products  293 us (8%)
  local copies, waits for them, and re-layouts  208 us (6%)
  blocking collectives  118 us (3%)
  other arithmetic  87 us (2%)
    reduce_scatter x1, waiting for transfers between devices, local(): lax.psum_scatter(gate_up_grad_full.astype(jnp.bfloat16), 'fsdp', scatter_...  541 us
    all_gather x1, waiting for transfers between devices, local(): lax.all_gather(qkv_weight, 'fsdp', axis=0, tiled=True)  413 us
    reduce_scatter x1, waiting for transfers between devices, local(): lax.psum_scatter(qkv_grad_full.astype(jnp.bfloat16), 'fsdp', scatter_dime...  407 us
    reduce_scatter x1, waiting for transfers between devices, local(): lax.psum_scatter(down_grad_full.astype(jnp.bfloat16), 'fsdp', scatter_dim...  231 us
    all_gather x1, waiting for transfers between devices, local(): lax.all_gather(gate_up_weight, 'fsdp', axis=1, tiled=True)  212 us
    all_gather x1, waiting for transfers between devices, local(): lax.all_gather(down_weight, 'fsdp', axis=1, tiled=True)  187 us
    all_to_all x1, waiting for transfers between devices, local(): lax.all_to_all(outgoing.reshape(experts, capacity, model_width), 'expert'...  169 us
    all_to_all x1, waiting for transfers between devices, local(): lax.all_to_all(grad_out.reshape(experts, capacity, model_width), 'expert'...  161 us
  transfers between devices with their start and end apart: 14, of which 13 were waited for; matrix products, arithmetic and copies ran while one was open for 12% of the time, Pallas kernels for 0%

commit v1 on v0

--- a/solution.py
+++ b/solution.py
@@ -1,3 +1,4 @@
+import functools
 import jax
 import jax.numpy as jnp
 from jax import lax
@@ -5,6 +6,29 @@
 
 EPSILON = 1e-06
 ROPE_BASE = 50000.0
+
+
+def produce_task(m, a_name):
+    odd = lax.axis_size(a_name)
+    a_next, right_arr, v1 = (odd, lax.axis_index(a_name), m.shape[0])
+    o_now, w1 = (m, 1)
+    while w1 < a_next:
+        o_now = jnp.concatenate(
+            [
+                o_now,
+                lax.ppermute(
+                    o_now,
+                    axis_name=a_name,
+                    perm=tuple(((b, (b - w1) % a_next) for b in range(a_next))),
+                ),
+            ],
+            axis=0,
+        )
+        w1 = 2 * w1
+    return jnp.roll(o_now, right_arr * v1, axis=0)
+
+
+_post_groups = functools.partial(produce_task, a_name="fsdp")
 
 
 def normalize(values):
@@ -65,7 +89,7 @@
     unit_one, factor_one = normalize(source)
     normed = (unit_one * attn_gain).astype(jnp.bfloat16)
     qkv_full, out_full, router_full = (
-        lax.all_gather(qkv_weight, "fsdp", axis=0, tiled=True),
+        _post_groups(qkv_weight),
         lax.all_gather(out_weight, "fsdp", axis=0, tiled=True),
         lax.all_gather(router_weight, "fsdp", axis=0, tiled=True),
     )

time: 3570 us -> 3840 us (1.076)
  blocking collectives: 118 us -> 912 us
  waiting for transfers between devices: 2810 us -> 2220 us
    all_gather x1, blocking collectives: 67.9 us -> 862 us  [local(): lax.all_gather(router_weight, 'fsdp', axis=0, tiled=True)]
    all_gather x1 -> x0, waiting for transfers between devices: 413 us -> none  [local(): lax.all_gather(qkv_weight, 'fsdp', axis=0, tiled=True)]
    ppermute x0 -> x3, waiting for transfers between devices: none -> 303 us  [produce_task(): lax.ppermute(o_now, axis_name=a_name, perm=tuple(((b, (b - w1) % a_next)...]
    all_gather x1, waiting for transfers between devices: 212 us -> 0.01 us  [local(): lax.all_gather(gate_up_weight, 'fsdp', axis=1, tiled=True)]
    all_gather x1, waiting for transfers between devices: 187 us -> 0.01 us  [local(): lax.all_gather(down_weight, 'fsdp', axis=1, tiled=True)]
    all_gather x1, waiting for transfers between devices: 83.1 us -> 0.02 us  [local(): lax.all_gather(out_weight, 'fsdp', axis=0, tiled=True)]
  transfers between devices with their start and end apart: 14 -> 16, of which waited for: 13 -> 11; matrix products, arithmetic and copies ran while one was open for 12% -> 12% of each run, Pallas kernels for 0% -> 0%
where the time goes in v1:
time: 3840 us; the launch traced here: 3830 us
  waiting for transfers between devices  2220 us (58%)
  blocking collectives  912 us (24%)
  matrix products  294 us (8%)
  local copies, waits for them, and re-layouts  245 us (6%)
  other arithmetic  97.4 us (3%)
    all_gather x1, blocking collectives, local(): lax.all_gather(router_weight, 'fsdp', axis=0, tiled=True)  862 us
    reduce_scatter x1, waiting for transfers between devices, local(): lax.psum_scatter(gate_up_grad_full.astype(jnp.bfloat16), 'fsdp', scatter_...  541 us
    reduce_scatter x1, waiting for transfers between devices, local(): lax.psum_scatter(qkv_grad_full.astype(jnp.bfloat16), 'fsdp', scatter_dime...  407 us
    ppermute x3, waiting for transfers between devices, produce_task(): lax.ppermute(o_now, axis_name=a_name, perm=tuple(((b, (b - w1) % a_next)...  303 us
    reduce_scatter x1, waiting for transfers between devices, local(): lax.psum_scatter(down_grad_full.astype(jnp.bfloat16), 'fsdp', scatter_dim...  230 us
    all_to_all x1, waiting for transfers between devices, local(): lax.all_to_all(outgoing.reshape(experts, capacity, model_width), 'expert'...  169 us
    all_to_all x1, waiting for transfers between devices, local(): lax.all_to_all(grad_out.reshape(experts, capacity, model_width), 'expert'...  161 us
    all_to_all x1, waiting for transfers between devices, local(): lax.all_to_all(input_rows, 'expert', split_axis=1, concat_axis=0, tiled=T...  130 us
  transfers between devices with their start and end apart: 16, of which 11 were waited for; matrix products, arithmetic and copies ran while one was open for 12% of the time, Pallas kernels for 0%

profile of v1, /device:TPU:0, one launch (start us, length us, event | category | flops | bytes accessed | tf_op | source)
XLA Modules:
  0.0 3825.9 jit_solution(5520466124504975319)
XLA Ops:
  15.0 122.3 %collective-permute-done = bf16[256,6144]{1,0:T(8,128)(2,1)S(1)} collective-permute-done((bf16[256,6144]{1,0:T(8,128)(2,1)S(1)}, bf16[256,6144]{1,0:T(8,128)(2,1)S(1)}, u32[]{:S(2)}, u32[]{:S(2)}) %collective-permute-start) | collective-permute-done | bytes 3145760 | tf_op jit(solution)/shard_map/ppermute | solution.py:19
  138.0 180.4 %collective-permute-done.1 = bf16[512,6144]{1,0:T(8,128)(2,1)S(1)} collective-permute-done((bf16[512,6144]{1,0:T(8,128)(2,1)S(1)}, bf16[512,6144]{1,0:T(8,128)(2,1)S(1)}, u32[]{:S(2)}, u32[]{:S(2)}) %collective-permute-start.1) | collective-permute-done | bytes 6291488 | tf_op jit(solution)/shard_map/ppermute | solution.py:19
  330.1 861.8 %all_gather.15 = bf16[2048,16]{0,1:T(8,128)(2,1)S(1)} all-gather(bf16[256,16]{0,1:T(8,128)(2,1)S(1)} %copy-done.69), channel_id=1, replica_groups=mesh['expert'=4,'fsdp'=8] {'fsdp'}, dimensions={0}, use_global_device_ids=true | all-gather | bytes 73728 | tf_op jit(solution)/shard_map/all_gather | solution.py:94
  1284.0 22.2 scatter_custom_fusion.1
  1335.4 160.8 %all-to-all-done.2 = bf16[16,256,2048]{2,1,0:T(8,128)(2,1)} async-done(((bf16[16,256,2048]{2,1,0:T(8,128)(2,1)}), bf16[16,256,2048]{2,1,0:T(8,128)(2,1)}, u32[]{:S(2)}, u32[]{:S(2)}) %all-to-all-start.2) | async-done | bytes 16777248 | tf_op jit(solution)/shard_map/all_to_all | solution.py:170
  1518.2 168.9 %all-to-all-done = bf16[16,256,2048]{2,1,0:T(8,128)(2,1)} async-done(((bf16[16,256,2048]{2,1,0:T(8,128)(2,1)}), bf16[16,256,2048]{2,1,0:T(8,128)(2,1)}, u32[]{:S(2)}, u32[]{:S(2)}) %all-to-all-start) | async-done | bytes 16777248 | tf_op jit(solution)/shard_map/all_to_all | solution.py:133
  1701.3 43.2 %fusion.57 = f32[4,1024,2048]{2,1,0:T(8,128)} fusion(bf16[4,1024,2048]{2,1,0:T(8,128)(2,1)} %bitcast.118, bf16[4,2048,2048]{2,1,0:T(8,128)(2,1)} %all-gather.6.cloned.1.call-done), kind=kOutput, calls=%fused_computation.152 | convolution fusion | flops 34359738368 | bytes 83886080 | tf_op jit(solution)/shard_map/erd,edf->erf/dot_general | solution.py:144
  1744.4 37.0 multiply_convert_fusion.1
  1781.4 27.3 convolution_convert_fusion.4
  1808.8 22.1 copy.196
  1837.9 43.4 %convolution_convert_fusion.2 = bf16[4,1024,2048]{2,1,0:T(8,128)(2,1)} fusion(bf16[4,2048,2048]{2,1,0:T(8,128)(2,1)} %all-gather.6.cloned.1.call-done, bf16[4,1024,1024]{2,1,0:T(8,128)(2,1)} %get-tuple-element.30, bf16[4,1024,1024]{2,1,0:T(8,128)(2,1)} %get-tuple-element.29), kind=kOutput, calls=%fused_computation.22 | convolution fusion | flops 34401681408 | bytes 67108864 | tf_op jit(solution)/shard_map/erf,edf->erd/dot_general | solution.py:193
  1881.3 22.1 copy.202
  1903.5 117.5 %all-to-all-done.1 = bf16[4,1024,2048]{2,0,1:T(4,128)(2,1)} async-done(((bf16[4,1024,2048]{2,0,1:T(4,128)(2,1)}), bf16[4,1024,2048]{2,0,1:T(4,128)(2,1)}, u32[]{:S(2)}, u32[]{:S(2)}) %all-to-all-start.1) | async-done | bytes 16777248 | tf_op jit(solution)/shard_map/all_to_all | solution.py:154
  2046.9 24.4 gather_fusion
  2081.1 130.2 %all-to-all-done.3 = bf16[4,1024,2048]{2,0,1:T(4,128)(2,1)} async-done(((bf16[4,1024,2048]{2,0,1:T(4,128)(2,1)}), bf16[4,1024,2048]{2,0,1:T(4,128)(2,1)}, u32[]{:S(2)}, u32[]{:S(2)}) %all-to-all-start.3) | async-done | bytes 16777248 | tf_op jit(solution)/shard_map/all_to_all | solution.py:196
  2229.9 24.7 gather_fusion.1
  2318.5 27.4 convolution_convert_fusion.3
  2346.0 81.7 %reduce-scatter.8.cloned.1.call-done = bf16[256,2048]{1,0:T(8,128)(2,1)} async-done(((bf16[2048,2048]{1,0:T(8,128)(2,1)}), bf16[256,2048]{1,0:T(8,128)(2,1)}) %reduce-scatter.8.cloned.1.call-update) | async-done | bytes 1048592 | tf_op jit(solution)/shard_map/reduce_scatter | solution.py:269
  2427.7 406.9 %reduce-scatter.6.cloned.1.call-done = bf16[256,6144]{1,0:T(8,128)(2,1)} async-done(((bf16[2048,6144]{1,0:T(8,128)(2,1)}), bf16[256,6144]{1,0:T(8,128)(2,1)}) %reduce-scatter.6.cloned.1.call-update) | async-done | bytes 3145744 | tf_op jit(solution)/shard_map/reduce_scatter | solution.py:266
  2834.6 43.8 %convolution_convert_fusion = bf16[4,2048,2048]{2,1,0:T(8,128)(2,1)} fusion(bf16[4,1024,2048]{2,1,0:T(8,128)(2,1)} %bitcast.119, bf16[4,1024,1024]{2,1,0:T(8,128)(2,1)} %get-tuple-element.30, bf16[4,1024,1024]{2,1,0:T(8,128)(2,1)} %get-tuple-element.29), kind=kOutput, calls=%fused_computation.4 | convolution fusion | flops 34410070016 | bytes 67108864 | tf_op jit(solution)/shard_map/erd,erf->edf/dot_general | solution.py:190
  2892.8 43.8 %all-reduce = (f32[2048]{0:T(1024)}, f32[128]{0:T(128)}, f32[128]{0:T(128)}, f32[2048]{0:T(1024)}) all-reduce(f32[2048]{0:T(1024)S(1)} %get-tuple-element.19, f32[128]{0:T(128)S(1)} %copy-done.74, f32[128]{0:T(128)S(1)} %copy-done.75, f32[2048]{0:T(1024)S(1)} %copy-done.59), channel_id=1, replica_groups=mesh['expert'=4,'fsdp'=8] {'expert','fsdp'}, use_global_device_ids=true, to_apply=%region_22.23 | all-reduce | flops 4352 | bytes 34816 | tf_op jit(solution)/shard_map/psum | solution.py:281
  2947.5 230.1 %reduce-scatter.14.cloned.1.call-done = bf16[4,128,2048]{2,1,0:T(8,128)(2,1)} async-done(((bf16[4,1024,2048]{2,1,0:T(8,128)(2,1)}), bf16[4,128,2048]{2,1,0:T(8,128)(2,1)}) %reduce-scatter.14.cloned.1.call-update) | async-done | bytes 2097168 | tf_op jit(solution)/shard_map/reduce_scatter | solution.py:203
  3181.8 83.1 %all-reduce.4.cloned.1.call-done = (bf16[256,6144]{1,0:T(8,128)(2,1)}, bf16[256,2048]{1,0:T(8,128)(2,1)}) async-done(((bf16[256,6144]{1,0:T(8,128)(2,1)}, bf16[256,2048]{1,0:T(8,128)(2,1)}), (bf16[256,6144]{1,0:T(8,128)(2,1)}, bf16[256,2048]{1,0:T(8,128)(2,1)})) %all-reduce.4.cloned.1.call-update) | async-done | bytes 4194320 | tf_op jit(solution)/shard_map/psum | solution.py:277
  3271.2 541.1 %reduce-scatter.12.cloned.1.call-done = bf16[4,256,2048]{2,1,0:T(8,128)(2,1)} async-done(((bf16[4,2048,2048]{2,1,0:T(8,128)(2,1)}), bf16[4,256,2048]{2,1,0:T(8,128)(2,1)}) %reduce-scatter.12.cloned.1.call-update) | async-done | bytes 4194320 | tf_op jit(solution)/shard_map/reduce_scatter | solution.py:200
  (279 shorter events, 344.3 us)
Async XLA Ops:
  7.2 1267.1 %all-gather.4.cloned.1.call-start = ((), (), s32[]{:S(2)}) async-start(), calls=%async_computation.9 | async-start | bytes 9437184 | tf_op jit(solution)/shard_map/all_gather | solution.py:93
  7.9 1693.3 %all-gather.6.cloned.1.call-start = ((), (), s32[]{:S(2)}) async-start(), calls=%async_computation.10 | async-start | bytes 37748736 | tf_op jit(solution)/shard_map/all_gather | solution.py:141
  9.1 128.3 %collective-permute-start = (bf16[256,6144]{1,0:T(8,128)(2,1)S(1)}, bf16[256,6144]{1,0:T(8,128)(2,1)S(1)}, u32[]{:S(2)}, u32[]{:S(2)}) collective-permute-start(bf16[256,6144]{1,0:T(8,128)(2,1)S(1)} %copy-done.3), channel_id=1, source_target_pairs={{0,7},{1,0},{2,1},{3,2},{4,3},{5,4},{6,5},{7,6},{8,15},{9,8},{10,9... | collective-permute-start | bytes 9437192 | tf_op jit(solution)/shard_map/ppermute | solution.py:19
  137.3 181.1 %copy-start.4 = (bf16[256,6144]{1,0:T(8,128)(2,1)}, bf16[256,6144]{1,0:T(8,128)(2,1)S(1)}, u32[]{:S(2)}) copy-start(bf16[256,6144]{1,0:T(8,128)(2,1)S(1)} %collective-permute-done) | copy-start | bytes 9437188
  137.9 189.0 %copy-start.57 = (s32[256,8]{0,1:T(8,128)S(1)}, s32[256,8]{0,1:T(8,128)}, u32[]{:S(2)}) copy-start(s32[256,8]{0,1:T(8,128)} %param.14) | copy-start | bytes 24580
  137.9 189.0 %copy-start.68 = (s32[256,8]{0,1:T(8,128)S(1)}, s32[256,8]{0,1:T(8,128)}, u32[]{:S(2)}) copy-start(s32[256,8]{0,1:T(8,128)} %param.15) | copy-start | bytes 24580
  137.9 192.1 %copy-start.69 = (bf16[256,16]{0,1:T(8,128)(2,1)S(1)}, bf16[256,16]{0,1:T(8,128)(2,1)}, u32[]{:S(2)}) copy-start(bf16[256,16]{0,1:T(8,128)(2,1)} %param.22) | copy-start | bytes 24580
  138.0 180.4 %collective-permute-start.1 = (bf16[512,6144]{1,0:T(8,128)(2,1)S(1)}, bf16[512,6144]{1,0:T(8,128)(2,1)S(1)}, u32[]{:S(2)}, u32[]{:S(2)}) collective-permute-start(bf16[512,6144]{1,0:T(8,128)(2,1)S(1)} %pad_maximum_fusion.4), channel_id=1, source_target_pairs={{0,6},{1,7},{2,0},{3,1},{4,2},{5,3},{6,4},{7,5},{8,14},{9,15},{10,... | collective-permute-start | bytes 18874376 | tf_op jit(solution)/shard_map/ppermute | solution.py:19
  325.4 876.4 %collective-permute-start.2 = (bf16[1024,6144]{1,0:T(8,128)(2,1)}, bf16[1024,6144]{1,0:T(8,128)(2,1)}, u32[]{:S(2)}, u32[]{:S(2)}) collective-permute-start(bf16[1024,6144]{1,0:T(8,128)(2,1)} %pad_maximum_fusion.1), channel_id=1, source_target_pairs={{0,4},{1,5},{2,6},{3,7},{4,0},{5,1},{6,2},{7,3},{8,12},{9,13},{10,... | collective-permute-start | bytes 37748744 | tf_op jit(solution)/shard_map/ppermute | solution.py:19
  330.1 866.7 %copy-start.5 = (bf16[256,6144]{1,0:T(8,128)(2,1)S(1)}, bf16[256,6144]{1,0:T(8,128)(2,1)}, u32[]{:S(2)}) copy-start(bf16[256,6144]{1,0:T(8,128)(2,1)} %copy-done.4) | copy-start | bytes 9437188
  1191.9 90.8 %copy-start.39 = (bf16[2048,16]{0,1:T(8,128)(2,1)}, bf16[2048,16]{0,1:T(8,128)(2,1)S(1)}, u32[]{:S(2)}) copy-start(bf16[2048,16]{0,1:T(8,128)(2,1)S(1)} %all_gather.15) | copy-start | bytes 196612
  1194.9 119.1 %copy-start.60 = (s32[2048,1]{0,1:T(1,128)}, s32[2048,1]{0,1:T(1,128)S(1)}, u32[]{:S(2)}) copy-start(s32[2048,1]{0,1:T(1,128)S(1)} %compare_select_fusion) | copy-start | bytes 24580
  1306.2 190.1 %all-to-all-start.2 = ((bf16[16,256,2048]{2,1,0:T(8,128)(2,1)}), bf16[16,256,2048]{2,1,0:T(8,128)(2,1)}, u32[]{:S(2)}, u32[]{:S(2)}) async-start(bf16[16,256,2048]{2,1,0:T(8,128)(2,1)} %bitcast.111), calls=%async_computation.2 | async-start | bytes 33554432 | tf_op jit(solution)/shard_map/all_to_all | solution.py:170
  1313.2 431.2 %all-gather.8.cloned.1.call-start = ((), (), s32[]{:S(2)}) async-start(), calls=%async_computation.11 | async-start | bytes 18874368 | tf_op jit(solution)/shard_map/all_gather | solution.py:142
  1496.3 190.9 %all-to-all-start = ((bf16[16,256,2048]{2,1,0:T(8,128)(2,1)}), bf16[16,256,2048]{2,1,0:T(8,128)(2,1)}, u32[]{:S(2)}, u32[]{:S(2)}) async-start(bf16[16,256,2048]{2,1,0:T(8,128)(2,1)} %bitcast.110), calls=%async_computation | async-start | bytes 33554432 | tf_op jit(solution)/shard_map/all_to_all | solution.py:133
  1830.9 190.1 %all-to-all-start.1 = ((bf16[4,1024,2048]{2,0,1:T(4,128)(2,1)}), bf16[4,1024,2048]{2,0,1:T(4,128)(2,1)}, u32[]{:S(2)}, u32[]{:S(2)}) async-start(bf16[4,1024,2048]{2,0,1:T(4,128)(2,1)} %copy.196), calls=%async_computation.1 | async-start | bytes 33554432 | tf_op jit(solution)/shard_map/all_to_all | solution.py:154
  1903.5 124.8 %copy-start.61 = (s32[2048,1]{0,1:T(1,128)S(1)}, s32[2048,1]{0,1:T(1,128)}, u32[]{:S(2)}) copy-start(s32[2048,1]{0,1:T(1,128)} %copy-done.60) | copy-start | bytes 24580
  2021.0 190.3 %all-to-all-start.3 = ((bf16[4,1024,2048]{2,0,1:T(4,128)(2,1)}), bf16[4,1024,2048]{2,0,1:T(4,128)(2,1)}, u32[]{:S(2)}, u32[]{:S(2)}) async-start(bf16[4,1024,2048]{2,0,1:T(4,128)(2,1)} %copy.202), calls=%async_computation.3 | async-start | bytes 33554432 | tf_op jit(solution)/shard_map/all_to_all | solution.py:196
  2028.2 399.5 %reduce-scatter.8.cloned.1.call-start = ((), (), s32[]{:S(2)}) async-start(), calls=%async_computation.13 | async-start | bytes 9437184 | tf_op jit(solution)/shard_map/reduce_scatter | solution.py:269
  2278.1 556.5 %reduce-scatter.6.cloned.1.call-start = ((), (), s32[]{:S(2)}) async-start(), calls=%async_computation.12 | async-start | bytes 28311552 | tf_op jit(solution)/shard_map/reduce_scatter | solution.py:266
  2316.3 623.8 %reduce-scatter.10.cloned.1.call-start = ((), (), s32[]{:S(2)}) async-start(), calls=%async_computation.14 | async-start | bytes 73728 | tf_op jit(solution)/shard_map/reduce_scatter | solution.py:272
  2318.4 859.2 %reduce-scatter.14.cloned.1.call-start = ((), (), s32[]{:S(2)}) async-start(), calls=%async_computation.16 | async-start | bytes 18874368 | tf_op jit(solution)/shard_map/reduce_scatter | solution.py:203
  2345.9 918.9 %all-reduce.4.cloned.1.call-start = ((), (), s32[]{:S(2)}) async-start(), calls=%async_computation.17 | async-start | bytes 8388608 | tf_op jit(solution)/shard_map/psum | solution.py:277
  2834.6 977.7 %reduce-scatter.12.cloned.1.call-start = ((), (), s32[]{:S(2)}) async-start(), calls=%async_computation.15 | async-start | bytes 37748736 | tf_op jit(solution)/shard_map/reduce_scatter | solution.py:200
  (70 other events, 524.8 us)
Sparse Core Ops, SparseCore 0:
  10.1 220.7 all-gather.3
  232.4 788.8 all-gather.5
  1316.2 229.7 all-gather.7
  2278.2 149.4 reduce-scatter.7
  2431.9 402.6 reduce-scatter.5
  2837.9 52.7 reduce-scatter.9
  2894.9 282.6 reduce-scatter.13
  3180.0 84.7 all-reduce.3
  3269.1 543.1 reduce-scatter.11
